TPU v7x, 256 devices: a whole 4x4x8 slice. The times are simulated.
256 devices in a mesh: aux: 2 (over core), row: 8 (over z), col: 16 (over x, y).
Axes of the slice: x: 4, y: 4, z: 8, core: 2. Of those that a mesh axis runs over, the one named last changes fastest.
Arguments:
- coulomb: bfloat16 [64, 2048, 2048], P('aux', 'row', 'col'), may hold values from -6 to 6
- occupied: bfloat16 [2048, 2048], P('row'), may hold values from -0.125 to 0.125
- virtual: bfloat16 [2048, 2048], P('row'), may hold values from -0.125 to 0.125
- tile_mask: int32 [16, 16], replicated, may hold values 0 or 1
Outputs:
- chi: float32 [64, 64], P('aux')
All inputs are finite; a program needn't handle non-finite values.
Results may differ from a plain program's by a relative error of at most 0.0042.
Values may be sent and summed in bfloat16 or wider, within the bound.
A program may use at most 128 MiB of HBM per device.

v0:
```python
import jax
import jax.numpy as jnp
from jax import lax
from jax.sharding import PartitionSpec as P

NAO = 2048
TILE = 128


def swapped(value, axis, apart):
    mask = 2**apart
    pairs = [(source, source ^ mask) for source in range(lax.axis_size(axis))]
    return lax.ppermute(value, axis, pairs)


def shards(coulomb, occupied, virtual, tile_mask):
    rows = lax.axis_size("row")
    cols = lax.axis_size("col")
    pdev, mrow, ncol = coulomb.shape
    nao = mrow * rows
    row_idx = lax.axis_index("row")
    col_idx = lax.axis_index("col")
    aux_idx = lax.axis_index("aux")
    tiles_r = mrow // TILE
    tiles_c = ncol // TILE
    local_tiles = lax.dynamic_slice(
        tile_mask, (row_idx * tiles_r, col_idx * tiles_c), (tiles_r, tiles_c)
    )
    local_mask = jnp.repeat(jnp.repeat(local_tiles, TILE, axis=0), TILE, axis=1).astype(
        jnp.bfloat16
    )
    screened = coulomb * local_mask[None]
    moved = lax.all_to_all(screened, "row", split_axis=0, concat_axis=1, tiled=True)
    pieces = moved.shape[0]
    occ_all, virt_all = (
        lax.all_gather(occupied, "row", axis=0, tiled=True),
        lax.all_gather(virtual, "row", axis=0, tiled=True),
    )
    half = jnp.einsum("ml,pmn->pln", occ_all, moved, preferred_element_type=jnp.float32).astype(
        jnp.bfloat16
    )
    jpart = mrow // cols
    shaped = half.reshape(pieces, rows, cols, jpart, ncol)
    spread = lax.all_to_all(shaped, "col", split_axis=2, concat_axis=4, tiled=True)
    spread = spread.reshape(pieces, rows * jpart, nao)
    dressed = jnp.einsum(
        "pln,ns->pls", spread, virt_all, preferred_element_type=jnp.float32
    ).astype(jnp.bfloat16)
    layered = dressed.reshape(pieces, rows, 1, jpart, cols, ncol)
    returned = lax.all_to_all(
        lax.all_to_all(layered, "row", split_axis=1, concat_axis=0, tiled=True),
        "col",
        split_axis=4,
        concat_axis=2,
        tiled=True,
    )
    aligned = returned.reshape(pdev, mrow, ncol)
    theirs = swapped(screened, "aux", 0)
    with_mine = jnp.einsum("pls,qls->pq", aligned, screened, preferred_element_type=jnp.float32)
    with_theirs = jnp.einsum("pls,qls->pq", aligned, theirs, preferred_element_type=jnp.float32)
    first_half = jnp.where(aux_idx == 0, with_mine, with_theirs)
    second_half = jnp.where(aux_idx == 0, with_theirs, with_mine)
    partial_chi = jnp.concatenate([first_half, second_half], axis=1)
    total_chi = lax.psum(partial_chi, ("row", "col"))
    return total_chi / NAO


def solution(mesh):
    placed = (P("aux", "row", "col"), P("row", None), P("row", None), P())
    return jax.shard_map(
        shards, mesh=mesh, in_specs=placed, out_specs=P("aux", None), check_vma=False
    )
```

profile of v0, /device:TPU:0, one launch (start us, length us, event | category | flops | bytes accessed | tf_op | source)
XLA Modules:
  0.0 1038.5 jit_solution(6755601709993652313)
XLA Ops:
  6.5 0.0 all-gather.3.cloned.1.call-start
  6.5 0.7 all-gather.3.cloned.1.call-update
  7.3 0.0 all-gather.5.cloned.1.call-start
  7.3 0.7 all-gather.5.cloned.1.call-update
  8.0 0.9 fusion.13
  8.9 0.1 broadcast_bitcast_fusion
  9.0 2.8 copy_multiply_fusion
  11.7 0.8 copy.15
  12.6 80.1 %all_to_all.66 = bf16[32,256,128]{2,1,0:T(8,128)(2,1)} all-to-all(bf16[32,256,128]{2,1,0:T(8,128)(2,1)S(1)} %copy.15), channel_id=1, replica_groups=mesh['aux'=2,'row'=8,'col'=16] {'row'}, dimensions={0} | all-to-all | bytes 4194304 | tf_op jit(solution)/shard_map/all_to_all | solution.py:33
  92.7 4.5 copy.16
  97.2 4.2 all_to_all.51
  101.4 45.5 %all-gather.3.cloned.1.call-done = bf16[2048,2048]{1,0:T(8,128)(2,1)} async-done(((bf16[256,2048]{1,0:T(8,128)(2,1)}), bf16[2048,2048]{1,0:T(8,128)(2,1)}) %all-gather.3.cloned.1.call-update) | async-done | bytes 8388624 | tf_op jit(solution)/shard_map/all_gather | solution.py:36
  146.9 9.8 fusion.10
  156.7 3.9 copy.17
  160.6 2.2 copy.18
  162.8 35.3 %all_to_all.67 = bf16[4,8,16,16,128]{4,3,1,0,2:T(8,128)(2,1)S(1)} all-to-all(bf16[4,8,16,16,128]{4,3,1,0,2:T(8,128)(2,1)S(1)} %copy.18), channel_id=1, replica_groups=mesh['aux'=2,'row'=8,'col'=16] {'col'}, dimensions={2} | all-to-all | bytes 4194304 | tf_op jit(solution)/shard_map/all_to_all | solution.py:44
  198.1 3.7 copy.19
  201.9 4.2 reshape.35
  206.0 35.8 %all-gather.5.cloned.1.call-done = bf16[2048,2048]{1,0:T(8,128)(2,1)} async-done(((bf16[256,2048]{1,0:T(8,128)(2,1)}), bf16[2048,2048]{1,0:T(8,128)(2,1)}) %all-gather.5.cloned.1.call-update) | async-done | bytes 8388624 | tf_op jit(solution)/shard_map/all_gather | solution.py:37
  241.9 8.5 fusion.7
  250.4 0.6 copy.23
  251.0 0.6 copy.20
  251.6 55.3 %all_to_all.68 = bf16[4,8,1,16,16,128]{5,4,3,0,2,1:T(8,128)(2,1)S(1)} all-to-all(bf16[4,8,1,16,16,128]{5,4,3,0,2,1:T(8,128)(2,1)S(1)} %copy.20), channel_id=1, replica_groups=mesh['aux'=2,'row'=8,'col'=16] {'row'}, dimensions={1} | all-to-all | bytes 4194304 | tf_op jit(solution)/shard_map/all_to_all | solution.py:51
  306.9 1.8 copy.21
  308.8 6.9 all-to-all-start.3
  315.6 0.1 collective-permute-start
  315.7 27.9 %all-to-all-done.3 = bf16[32,1,1,16,16,128]{5,3,0,2,1,4:T(8,128)(2,1)} async-done(((bf16[32,1,1,16,16,128]{5,3,0,2,1,4:T(8,128)(2,1)}), bf16[32,1,1,16,16,128]{5,3,0,2,1,4:T(8,128)(2,1)}, u32[]{:S(2)}, u32[]{:S(2)}) %all-to-all-start.3) | async-done | bytes 2097184 | tf_op jit(solution)/shard_map/all_to_all | solution.py:50
  343.7 2.1 copy.22
  345.8 0.7 convolution_bitcast_fusion.1
  346.5 0.0 collective-permute-done
  346.5 2.3 broadcast_select_fusion.1
  348.8 0.1 pad_maximum_fusion
  348.9 682.2 %psum.7 = f32[32,64]{1,0:T(8,128)S(1)} all-reduce(f32[32,64]{1,0:T(8,128)S(1)} %pad_maximum_fusion), channel_id=1, replica_groups=mesh['aux'=2,'row'=8,'col'=16] {'row','col'}, use_global_device_ids=true, to_apply=%region_0.1 | all-reduce | flops 2048 | bytes 16384 | tf_op jit(solution)/shard_map/psum | solution.py:64
  1031.1 0.6 broadcast_multiply_fusion
Async XLA Ops:
  6.5 140.3 %all-gather.3.cloned.1.call-start = ((), (), s32[]{:S(2)}) async-start(), calls=%async_computation.4 | async-start | bytes 9437184 | tf_op jit(solution)/shard_map/all_gather | solution.py:36
  7.3 234.6 %all-gather.5.cloned.1.call-start = ((), (), s32[]{:S(2)}) async-start(), calls=%async_computation.5 | async-start | bytes 9437184 | tf_op jit(solution)/shard_map/all_gather | solution.py:37
  308.8 34.9 %all-to-all-start.3 = ((bf16[32,1,1,16,16,128]{5,3,0,2,1,4:T(8,128)(2,1)}), bf16[32,1,1,16,16,128]{5,3,0,2,1,4:T(8,128)(2,1)}, u32[]{:S(2)}, u32[]{:S(2)}) async-start(bf16[32,1,1,16,16,128]{5,3,0,2,1,4:T(8,128)(2,1)} %copy.21), calls=%async_computation.3 | async-start | bytes 4194304 | tf_op jit(solution)/shard_map/all_to_all | solution.py:50
  315.6 30.8 %collective-permute-start = (bf16[32,256,128]{2,0,1:T(8,128)(2,1)S(1)}, bf16[32,256,128]{2,0,1:T(8,128)(2,1)}, u32[]{:S(2)}, u32[]{:S(2)}) collective-permute-start(bf16[32,256,128]{2,0,1:T(8,128)(2,1)S(1)} %copy_multiply_fusion), channel_id=1, source_target_pairs={{0,128},{128,0},{1,129},{129,1},{2,130},{130,2},{3,131},{131,3},{4... | collective-permute-start | bytes 6291464 | tf_op jit(solution)/shard_map/ppermute | solution.py:13
Sparse Core Ops, SparseCore 0:
  9.1 137.6 all-gather.2
  148.7 93.1 all-gather.4
where the time goes:
time: 1040 us
  blocking collectives  853 us (82%)
  waiting for transfers between devices  111 us (11%)
  local copies, waits for them, and re-layouts  28.8 us (3%)
  matrix products  21.3 us (2%)
  between operations  13.5 us (1%)
    psum x1, blocking collectives, shards(): total_chi = lax.psum(partial_chi, ('row', 'col'))  682 us
    all_to_all x1, blocking collectives, shards(): lax.all_to_all(screened, 'row', split_axis=0, concat_axis=1, tiled=True)  80.1 us
    all_to_all x1, blocking collectives, shards(): lax.all_to_all(layered, 'row', split_axis=1, concat_axis=0, tiled=True)  55.3 us
    all_gather x1, waiting for transfers between devices, shards(): lax.all_gather(occupied, 'row', axis=0, tiled=True)  45.5 us
    all_gather x1, waiting for transfers between devices, shards(): lax.all_gather(virtual, 'row', axis=0, tiled=True)  35.8 us
    all_to_all x1, blocking collectives, shards(): lax.all_to_all(shaped, 'col', split_axis=2, concat_axis=4, tiled=True)  35.3 us
    all_to_all x1, waiting for transfers between devices, shards(): lax.all_to_all(lax.all_to_all(layered, 'row', split_axis=1, concat_axis=0...  27.9 us
  transfers between devices with their start and end apart: 4, of which 3 were waited for; matrix products, arithmetic and copies ran while one was open for 3% of the time, Pallas kernels for 0%

commit v1 on v0

--- a/solution.py
+++ b/solution.py
@@ -61,7 +61,7 @@
     first_half = jnp.where(aux_idx == 0, with_mine, with_theirs)
     second_half = jnp.where(aux_idx == 0, with_theirs, with_mine)
     partial_chi = jnp.concatenate([first_half, second_half], axis=1)
-    total_chi = lax.psum(partial_chi, ("row", "col"))
+    total_chi = lax.psum(lax.psum(partial_chi, "row"), "col")
     return total_chi / NAO
 
 

time: 1040 us -> 455 us (0.44)
  blocking collectives: 853 us -> 269 us
    psum x1 -> x2, blocking collectives: 682 us -> 98.3 us  [shards(): total_chi = lax.psum(lax.psum(partial_chi, 'row'), 'col')]
  transfers between devices with their start and end apart: 4 -> 4, of which waited for: 3 -> 3; matrix products, arithmetic and copies ran while one was open for 3% -> 8% of each run, Pallas kernels for 0% -> 0%
where the time goes in v1:
time: 455 us
  blocking collectives  269 us (59%)
  waiting for transfers between devices  111 us (24%)
  local copies, waits for them, and re-layouts  28.8 us (6%)
  matrix products  21.3 us (5%)
  between operations  13.5 us (3%)
  starting transfers between devices  6.99 us (2%)
    psum x2, blocking collectives, shards(): total_chi = lax.psum(lax.psum(partial_chi, 'row'), 'col')  98.3 us
    all_to_all x1, blocking collectives, shards(): lax.all_to_all(screened, 'row', split_axis=0, concat_axis=1, tiled=True)  80.1 us
    all_to_all x1, blocking collectives, shards(): lax.all_to_all(layered, 'row', split_axis=1, concat_axis=0, tiled=True)  55.3 us
    all_gather x1, waiting for transfers between devices, shards(): lax.all_gather(occupied, 'row', axis=0, tiled=True)  45.5 us
    all_gather x1, waiting for transfers between devices, shards(): lax.all_gather(virtual, 'row', axis=0, tiled=True)  35.7 us
    all_to_all x1, blocking collectives, shards(): lax.all_to_all(shaped, 'col', split_axis=2, concat_axis=4, tiled=True)  35.4 us
    all_to_all x1, waiting for transfers between devices, shards(): lax.all_to_all(lax.all_to_all(layered, 'row', split_axis=1, concat_axis=0...  27.9 us
    dot_general x1, matrix products, shards(): jnp.einsum('ml,pmn->pln', occ_all, moved, preferred_element_type=jnp.floa...  9.81 us
  transfers between devices with their start and end apart: 4, of which 3 were waited for; matrix products, arithmetic and copies ran while one was open for 8% of the time, Pallas kernels for 0%

profile of v1, /device:TPU:0, one launch (start us, length us, event | category | flops | bytes accessed | tf_op | source)
XLA Modules:
  0.0 454.6 jit_solution(17523791207048425931)
XLA Ops:
  6.5 0.0 all-gather.3.cloned.1.call-start
  6.5 0.7 all-gather.3.cloned.1.call-update
  7.3 0.0 all-gather.5.cloned.1.call-start
  7.3 0.7 all-gather.5.cloned.1.call-update
  8.0 0.9 fusion.13
  8.9 0.1 broadcast_bitcast_fusion
  9.0 2.8 copy_multiply_fusion
  11.7 0.8 copy.15
  12.6 80.1 %all_to_all.66 = bf16[32,256,128]{2,1,0:T(8,128)(2,1)} all-to-all(bf16[32,256,128]{2,1,0:T(8,128)(2,1)S(1)} %copy.15), channel_id=1, replica_groups=mesh['aux'=2,'row'=8,'col'=16] {'row'}, dimensions={0} | all-to-all | bytes 4194304 | tf_op jit(solution)/shard_map/all_to_all | solution.py:33
  92.7 4.5 copy.16
  97.2 4.2 all_to_all.51
  101.4 45.5 %all-gather.3.cloned.1.call-done = bf16[2048,2048]{1,0:T(8,128)(2,1)} async-done(((bf16[256,2048]{1,0:T(8,128)(2,1)}), bf16[2048,2048]{1,0:T(8,128)(2,1)}) %all-gather.3.cloned.1.call-update) | async-done | bytes 8388624 | tf_op jit(solution)/shard_map/all_gather | solution.py:36
  146.9 9.8 %fusion.10 = bf16[4,2048,128]{1,2,0:T(8,128)(2,1)} fusion(bf16[4,2048,128]{1,2,0:T(8,128)(2,1)} %all_to_all.51, bf16[2048,2048]{1,0:T(8,128)(2,1)} %all-gather.3.cloned.1.call-done), kind=kOutput, calls=%fused_computation.6 | convolution fusion | flops 4296015872 | bytes 12582912 | tf_op jit(solution)/shard_map/ml,pmn->pln/dot_general | solution.py:39
  156.7 3.9 copy.17
  160.6 2.2 copy.18
  162.8 35.4 %all_to_all.67 = bf16[4,8,16,16,128]{4,3,1,0,2:T(8,128)(2,1)S(1)} all-to-all(bf16[4,8,16,16,128]{4,3,1,0,2:T(8,128)(2,1)S(1)} %copy.18), channel_id=1, replica_groups=mesh['aux'=2,'row'=8,'col'=16] {'col'}, dimensions={2} | all-to-all | bytes 4194304 | tf_op jit(solution)/shard_map/all_to_all | solution.py:44
  198.2 3.7 copy.19
  202.0 4.2 reshape.35
  206.2 35.7 %all-gather.5.cloned.1.call-done = bf16[2048,2048]{1,0:T(8,128)(2,1)} async-done(((bf16[256,2048]{1,0:T(8,128)(2,1)}), bf16[2048,2048]{1,0:T(8,128)(2,1)}) %all-gather.5.cloned.1.call-update) | async-done | bytes 8388624 | tf_op jit(solution)/shard_map/all_gather | solution.py:37
  241.9 8.5 %fusion.7 = bf16[4,128,2048]{2,1,0:T(8,128)(2,1)S(1)} fusion(bf16[4,128,2048]{2,1,0:T(8,128)(2,1)} %reshape.35, bf16[2048,2048]{1,0:T(8,128)(2,1)} %all-gather.5.cloned.1.call-done), kind=kOutput, calls=%fused_computation.5 | convolution fusion | flops 4296015872 | bytes 12582912 | tf_op jit(solution)/shard_map/pln,ns->pls/dot_general | solution.py:46
  250.4 0.6 copy.23
  251.0 0.6 copy.20
  251.6 55.3 %all_to_all.68 = bf16[4,8,1,16,16,128]{5,4,3,0,2,1:T(8,128)(2,1)S(1)} all-to-all(bf16[4,8,1,16,16,128]{5,4,3,0,2,1:T(8,128)(2,1)S(1)} %copy.20), channel_id=1, replica_groups=mesh['aux'=2,'row'=8,'col'=16] {'row'}, dimensions={1} | all-to-all | bytes 4194304 | tf_op jit(solution)/shard_map/all_to_all | solution.py:51
  306.9 1.8 copy.21
  308.8 6.9 %all-to-all-start.3 = ((bf16[32,1,1,16,16,128]{5,3,0,2,1,4:T(8,128)(2,1)}), bf16[32,1,1,16,16,128]{5,3,0,2,1,4:T(8,128)(2,1)}, u32[]{:S(2)}, u32[]{:S(2)}) async-start(bf16[32,1,1,16,16,128]{5,3,0,2,1,4:T(8,128)(2,1)} %copy.21), calls=%async_computation.3 | async-start | bytes 4194304 | tf_op jit(solution)/shard_map/all_to_all | solution.py:50
  315.6 0.1 collective-permute-start
  315.7 27.9 %all-to-all-done.3 = bf16[32,1,1,16,16,128]{5,3,0,2,1,4:T(8,128)(2,1)} async-done(((bf16[32,1,1,16,16,128]{5,3,0,2,1,4:T(8,128)(2,1)}), bf16[32,1,1,16,16,128]{5,3,0,2,1,4:T(8,128)(2,1)}, u32[]{:S(2)}, u32[]{:S(2)}) %all-to-all-start.3) | async-done | bytes 2097184 | tf_op jit(solution)/shard_map/all_to_all | solution.py:50
  343.7 2.1 copy.22
  345.8 0.7 convolution_bitcast_fusion.1
  346.5 0.0 collective-permute-done
  346.5 2.3 broadcast_select_fusion.1
  348.8 0.1 pad_maximum_fusion
  348.9 27.2 %psum.14 = f32[32,64]{1,0:T(8,128)S(1)} all-reduce(f32[32,64]{1,0:T(8,128)S(1)} %pad_maximum_fusion), channel_id=1, replica_groups=mesh['aux'=2,'row'=8,'col'=16] {'row'}, use_global_device_ids=true, to_apply=%region_0.1 | all-reduce | flops 2048 | bytes 16384 | tf_op jit(solution)/shard_map/psum | solution.py:64
  376.1 71.1 %psum.15 = f32[32,64]{1,0:T(8,128)S(1)} all-reduce(f32[32,64]{1,0:T(8,128)S(1)} %psum.14), channel_id=1, replica_groups=mesh['aux'=2,'row'=8,'col'=16] {'col'}, use_global_device_ids=true, to_apply=%region_1.2 | all-reduce | flops 2048 | bytes 16384 | tf_op jit(solution)/shard_map/psum | solution.py:64
  447.1 0.6 broadcast_multiply_fusion
Async XLA Ops:
  6.5 140.3 %all-gather.3.cloned.1.call-start = ((), (), s32[]{:S(2)}) async-start(), calls=%async_computation.4 | async-start | bytes 9437184 | tf_op jit(solution)/shard_map/all_gather | solution.py:36
  7.3 234.6 %all-gather.5.cloned.1.call-start = ((), (), s32[]{:S(2)}) async-start(), calls=%async_computation.5 | async-start | bytes 9437184 | tf_op jit(solution)/shard_map/all_gather | solution.py:37
  308.8 34.9 %all-to-all-start.3 = ((bf16[32,1,1,16,16,128]{5,3,0,2,1,4:T(8,128)(2,1)}), bf16[32,1,1,16,16,128]{5,3,0,2,1,4:T(8,128)(2,1)}, u32[]{:S(2)}, u32[]{:S(2)}) async-start(bf16[32,1,1,16,16,128]{5,3,0,2,1,4:T(8,128)(2,1)} %copy.21), calls=%async_computation.3 | async-start | bytes 4194304 | tf_op jit(solution)/shard_map/all_to_all | solution.py:50
  315.6 30.8 %collective-permute-start = (bf16[32,256,128]{2,0,1:T(8,128)(2,1)S(1)}, bf16[32,256,128]{2,0,1:T(8,128)(2,1)}, u32[]{:S(2)}, u32[]{:S(2)}) collective-permute-start(bf16[32,256,128]{2,0,1:T(8,128)(2,1)S(1)} %copy_multiply_fusion), channel_id=1, source_target_pairs={{0,128},{128,0},{1,129},{129,1},{2,130},{130,2},{3,131},{131,3},{4... | collective-permute-start | bytes 6291464 | tf_op jit(solution)/shard_map/ppermute | solution.py:13
Sparse Core Ops, SparseCore 0:
  9.1 137.6 all-gather.2
  148.7 93.1 all-gather.4
